TPU v7x, 512 devices: a whole 4x8x8 slice. The times are simulated.
512 devices in a mesh: ctx: 64 (over x, z, core), kvh: 8 (over y).
Axes of the slice: x: 4, y: 8, z: 8, core: 2. Of those that a mesh axis runs over, the one named last changes fastest.
Arguments:
- queries: bfloat16 [32768, 8192], P('ctx', 'kvh')
- key_vector_rows: bfloat16 [32768, 1024], P('ctx', 'kvh')
- value_vector_rows: bfloat16 [32768, 1024], P('ctx', 'kvh'), may hold values from -6 to 6
- block_picks: int32 [256, 8], P('ctx'), may hold values from 0 to 255, as said below
Outputs:
- attended: bfloat16 [32768, 8192], P(('ctx', 'kvh'))
Inputs may be any that keep to these rules, and one draw needn't show every extreme that they name: block_picks[b, 0] = b. The other entries of a row name 7 distinct blocks that lie on other indices of ctx (block c lies on index c // 4). Over the 4 rows of one index of ctx, the entries naming blocks of any one other index are at most 2 and name at most 1 distinct blocks; both bounds are reached in every draw.
All inputs are finite; a program needn't handle non-finite values.
Results may differ from a plain program's by a relative error of at most 0.0047.
Values may be sent and summed in bfloat16 or wider, within the bound.
No kernel may reach another device: no remote copies, remote signals or barrier semaphores. Data moves between devices by JAX's collectives and lax.ppermute only.
A program may use at most 64 MiB of HBM per device.

v0:
```python
import math
import jax
import jax.numpy as jnp
from jax import lax
from jax.sharding import PartitionSpec as P

HEAD_SIZE = 128
BLOCK_TOKENS = 128
PICKED_BLOCKS = 8


def plan_each(remote, blocks, peer_count, capacity):
    flat_picks = remote.reshape(-1)
    owners = flat_picks // blocks
    local_ids = flat_picks % blocks
    owner_hits = (owners[:, None] == jnp.arange(peer_count, dtype=jnp.int32)[None, :]).astype(
        jnp.int32
    )
    running = jnp.cumsum(owner_hits, axis=0) * owner_hits
    slot_rank = jnp.sum(running, axis=1) - 1
    slot_hits = (slot_rank[:, None] == jnp.arange(capacity, dtype=jnp.int32)[None, :]).astype(
        jnp.int32
    )
    requests = jnp.dot((owner_hits * local_ids[:, None]).T, slot_hits)
    return (requests, slot_rank)


def block_attention(query_block, kv_block, kv_heads):
    block_len = query_block.shape[0]
    pick_count = kv_block.shape[0]
    group_size = query_block.shape[1] // (kv_heads * HEAD_SIZE)
    query_heads = query_block.reshape(block_len, kv_heads, group_size, HEAD_SIZE)
    stacked = kv_block.reshape(pick_count * block_len, 2, kv_heads, HEAD_SIZE)
    key_selection = stacked[:, 0]
    value_selection = stacked[:, 1]
    scores = jnp.einsum(
        "qgxd,kgd->gxqk", query_heads, key_selection, preferred_element_type=jnp.float32
    )
    scores = scores * (1.0 / math.sqrt(HEAD_SIZE))
    positions = jnp.arange(block_len, dtype=jnp.int32)
    causal = positions[None, :] <= positions[:, None]
    visible = jnp.concatenate(
        [causal, jnp.ones((block_len, (pick_count - 1) * block_len), dtype=bool)], axis=1
    )
    scores = jnp.where(visible, scores, -jnp.inf)
    row_max = jnp.max(scores, axis=-1, keepdims=True)
    exponents = jnp.exp(scores - row_max)
    totals = jnp.sum(exponents, axis=-1, keepdims=True)
    weights = exponents.astype(jnp.bfloat16)
    blended = jnp.einsum(
        "gxqk,kgd->qgxd", weights, value_selection, preferred_element_type=jnp.float32
    )
    blended = blended / jnp.transpose(totals, (2, 0, 1, 3))
    return blended.reshape(block_len, -1).astype(jnp.bfloat16)


def body(queries, key_vector_rows, value_vector_rows, block_picks):
    peer_count = lax.axis_size("ctx")
    my_index = lax.axis_index("ctx")
    tok_dev = key_vector_rows.shape[0]
    blocks = tok_dev // BLOCK_TOKENS
    kv_heads = key_vector_rows.shape[1] // HEAD_SIZE
    local_kv = jnp.concatenate([key_vector_rows, value_vector_rows], axis=1).reshape(
        blocks, BLOCK_TOKENS, 2 * kv_heads * HEAD_SIZE
    )
    remote = block_picks[:, 1:]
    far_count = blocks * (PICKED_BLOCKS - 1)
    distinct_cap = (far_count // 2 + peer_count - 2) // (peer_count - 1)
    capacity = 2 * distinct_cap
    requests, slot_rank = plan_each(remote, blocks, peer_count, capacity)
    pick_table = lax.all_gather(block_picks, "ctx", axis=0, tiled=True)
    all_rows = pick_table[:, 1:].reshape(peer_count, blocks, PICKED_BLOCKS - 1)

    def requests_of(rows_one):
        return plan_each(rows_one, blocks, peer_count, capacity)[0]

    all_requests = jax.vmap(requests_of)(all_rows)
    wanted = jnp.take(all_requests, my_index, axis=1)
    outgoing = local_kv[wanted]
    incoming = lax.all_to_all(outgoing, "ctx", split_axis=0, concat_axis=0, tiled=True)
    owners = (remote // blocks).reshape(-1)
    fetched = incoming.reshape(peer_count * capacity, BLOCK_TOKENS, -1)[
        owners * capacity + slot_rank
    ]
    fetched = fetched.reshape(blocks, PICKED_BLOCKS - 1, BLOCK_TOKENS, -1)
    chosen = jnp.concatenate([local_kv[:, None], fetched], axis=1)

    def attend_pair(pair):
        return block_attention(pair[0], pair[1], kv_heads)

    attended = lax.map(attend_pair, (queries.reshape(blocks, BLOCK_TOKENS, -1), chosen))
    attended = attended.reshape(tok_dev, -1)
    return lax.all_to_all(attended, "kvh", split_axis=0, concat_axis=1, tiled=True)


def solution(mesh):
    return jax.shard_map(
        body,
        mesh=mesh,
        in_specs=(P("ctx", "kvh"), P("ctx", "kvh"), P("ctx", "kvh"), P("ctx", None)),
        out_specs=P(("ctx", "kvh"), None),
        check_vma=False,
    )
```

profile of v0, /device:TPU:1, one launch (start us, length us, event | category | flops | bytes accessed | tf_op | source)
XLA Modules:
  0.0 326.1 jit_solution(9920349787377583914)
XLA Ops:
  0.0 57.4 %all-gather = s32[64,4,8]{2,1,0:T(4,128)S(1)} all-gather(s32[1,4,8]{2,1,0:T(4,128)} %bitcast.120), channel_id=1, replica_groups=mesh['ctx'=64,'kvh'=8] {'ctx'}, dimensions={0}, use_global_device_ids=true | all-gather | bytes 8320 | tf_op jit(solution)/shard_map/all_gather | solution.py:71
  57.7 1.3 select_reduce_fusion
  59.1 2.6 fusion.19
  61.9 0.1 reshape.245
  62.2 6.3 %gather_fusion = bf16[128,128,256]{2,1,0:T(8,128)(2,1)} fusion(bf16[4,128,256]{2,1,0:T(8,128)(2,1)S(1)} %bitcast.108, s32[1024]{0:T(1024)S(1)} %pad_clamp_fusion.1), kind=kCustom, calls=%fused_computation | custom fusion | bytes 16777728 | tf_op jit(solution)/shard_map/gather | solution.py:79
  68.5 5.9 %all-to-all-start = ((bf16[64,2,128,256]{3,2,1,0:T(8,128)(2,1)}), bf16[64,2,128,256]{3,2,1,0:T(8,128)(2,1)}, u32[]{:S(2)}, u32[]{:S(2)}) async-start(bf16[64,2,128,256]{3,2,1,0:T(8,128)(2,1)} %bitcast.110), calls=%async_computation | async-start | bytes 16777216 | tf_op jit(solution)/shard_map/all_to_all | solution.py:80
  74.8 0.2 select_reduce_fusion.1
  75.0 185.1 %all-to-all-done = bf16[64,2,128,256]{3,2,1,0:T(8,128)(2,1)} async-done(((bf16[64,2,128,256]{3,2,1,0:T(8,128)(2,1)}), bf16[64,2,128,256]{3,2,1,0:T(8,128)(2,1)}, u32[]{:S(2)}, u32[]{:S(2)}) %all-to-all-start) | async-done | bytes 8388640 | tf_op jit(solution)/shard_map/all_to_all | solution.py:80
  260.1 5.4 %gather_fusion.1 = bf16[28,128,256]{2,1,0:T(8,128)(2,1)} fusion(bf16[128,128,256]{2,1,0:T(8,128)(2,1)} %bitcast.22, s32[1024]{0:T(1024)S(1)} %pad_clamp_fusion), kind=kCustom, calls=%fused_computation.1 | custom fusion | bytes 3670128 | tf_op jit(solution)/shard_map/gather | solution.py:82
  265.5 1.7 pad_maximum_fusion
  267.2 21.8 %while.11 = (s32[]{:T(128)}, bf16[4,128,1024]{2,1,0:T(8,128)(2,1)}, bf16[4,8,128,256]{3,2,1,0:T(8,128)(2,1)S(1)}, bf16[4,128,1024]{2,1,0:T(8,128)(2,1)}, s32[]{:T(128)}, /*index=5*/pred[]{:T(512)}) while((s32[]{:T(128)}, bf16[4,128,1024]{2,1,0:T(8,128)(2,1)}, bf16[4,8,128,256]{3,2,1,0:T(8,128)(2,1)S(1)}, bf16[4,128,1024]{2,1,0:T(8,128)(2,1)}, ...), condition=%wide.region_7.8_spmd, body=%wide.region_4.7_spmd.sunk | while | flops 548681728 | bytes 19452492 | solution.py:91
  267.2 0.1 reshape.266
  267.4 0.4 copy.68
  267.8 1.0 constant_dynamic-slice_fusion.4
  268.8 0.2 copy.67
  269.0 0.7 fusion.44
  269.8 0.9 fusion.45
  270.6 1.1 fusion.46
  271.8 0.1 copy.69
  271.9 0.7 constant_dynamic-update-slice_fusion.4
  272.7 0.1 reshape.266
  272.8 0.4 copy.68
  273.2 1.0 constant_dynamic-slice_fusion.4
  274.2 0.2 copy.67
  274.4 0.7 fusion.44
  275.2 0.9 fusion.45
  276.1 1.1 fusion.46
  277.2 0.1 copy.69
  277.3 0.7 constant_dynamic-update-slice_fusion.4
  278.1 0.1 reshape.266
  278.2 0.4 copy.68
  278.7 1.0 constant_dynamic-slice_fusion.4
  279.6 0.2 copy.67
  279.9 0.7 fusion.44
  280.6 0.9 fusion.45
  281.5 1.1 fusion.46
  282.6 0.1 copy.69
  282.8 0.7 constant_dynamic-update-slice_fusion.4
  283.7 0.4 copy.68
  284.1 1.0 constant_dynamic-slice_fusion.4
  285.1 0.2 copy.67
  285.3 0.7 fusion.44
  286.1 0.9 fusion.45
  286.9 1.1 fusion.46
  288.1 0.1 copy.69
  288.2 0.7 constant_dynamic-update-slice_fusion.4
  289.0 36.1 %all_to_all.24 = bf16[8,64,1024]{2,1,0:T(8,128)(2,1)S(1)} all-to-all(bf16[8,64,1024]{2,1,0:T(8,128)(2,1)} %bitcast.117), channel_id=1, replica_groups=mesh['ctx'=64,'kvh'=8] {'kvh'}, dimensions={0} | all-to-all | bytes 2097152 | tf_op jit(solution)/shard_map/all_to_all | solution.py:93
  325.0 1.1 copy.61
  (41 shorter events, 1.6 us)
Async XLA Ops:
  0.0 62.1 %copy-start = (bf16[512,128]{1,0:T(8,128)(2,1)S(1)}, bf16[512,128]{1,0:T(8,128)(2,1)}, u32[]{:S(2)}) copy-start(bf16[512,128]{1,0:T(8,128)(2,1)} %param.7) | copy-start | bytes 393220
  0.0 62.1 %copy-start.1 = (bf16[512,128]{1,0:T(8,128)(2,1)S(1)}, bf16[512,128]{1,0:T(8,128)(2,1)}, u32[]{:S(2)}) copy-start(bf16[512,128]{1,0:T(8,128)(2,1)} %param.8) | copy-start | bytes 393220
  68.5 5.9 %copy-start.2 = (s32[4,8]{1,0:T(4,128)S(1)}, s32[4,8]{1,0:T(4,128)}, u32[]{:S(2)}) copy-start(s32[4,8]{1,0:T(4,128)} %param.9) | copy-start | bytes 388
  68.5 191.6 %all-to-all-start = ((bf16[64,2,128,256]{3,2,1,0:T(8,128)(2,1)}), bf16[64,2,128,256]{3,2,1,0:T(8,128)(2,1)}, u32[]{:S(2)}, u32[]{:S(2)}) async-start(bf16[64,2,128,256]{3,2,1,0:T(8,128)(2,1)} %bitcast.110), calls=%async_computation | async-start | bytes 16777216 | tf_op jit(solution)/shard_map/all_to_all | solution.py:80
where the time goes:
time: 327 us; the launch traced here: 326 us
  waiting for transfers between devices  185 us (57%)
  blocking collectives  93.5 us (29%)
  local copies, waits for them, and re-layouts  24.2 us (7%)
  matrix products  10.1 us (3%)
  other arithmetic  6.97 us (2%)
  starting transfers between devices  5.87 us (2%)
    all_to_all x1, waiting for transfers between devices, body(): lax.all_to_all(outgoing, 'ctx', split_axis=0, concat_axis=0, tiled=True)  185 us
    all_gather x1, blocking collectives, body(): pick_table = lax.all_gather(block_picks, 'ctx', axis=0, tiled=True)  57.4 us
    all_to_all x1, blocking collectives, body(): lax.all_to_all(attended, 'kvh', split_axis=0, concat_axis=1, tiled=True)  36.1 us
  transfers between devices with their start and end apart: 1, of which 1 were waited for; matrix products, arithmetic and copies ran while one was open for 0% of the time, Pallas kernels for 0%

commit v1 on v0

--- a/solution.py
+++ b/solution.py
@@ -68,7 +68,8 @@
     distinct_cap = (far_count // 2 + peer_count - 2) // (peer_count - 1)
     capacity = 2 * distinct_cap
     requests, slot_rank = plan_each(remote, blocks, peer_count, capacity)
-    pick_table = lax.all_gather(block_picks, "ctx", axis=0, tiled=True)
+    sent = jnp.stack([block_picks] * lax.axis_size("ctx"))
+    pick_table = jnp.concatenate(lax.all_to_all(sent, "ctx", 0, 0), axis=0)
     all_rows = pick_table[:, 1:].reshape(peer_count, blocks, PICKED_BLOCKS - 1)
 
     def requests_of(rows_one):

time: 327 us -> 295 us (0.902)
  blocking collectives: 93.5 us -> 36.1 us
  starting transfers between devices: 5.87 us -> 20.4 us
  waiting for transfers between devices: 185 us -> 194 us
    all_gather x1 -> x0, blocking collectives: 57.4 us -> none  [body(): pick_table = lax.all_gather(block_picks, 'ctx', axis=0, tiled=True)]
    all_to_all x0 -> x1, starting transfers between devices: none -> 14.8 us  [body(): pick_table = jnp.concatenate(lax.all_to_all(sent, 'ctx', 0, 0), axis=0)]
    all_to_all x0 -> x1, waiting for transfers between devices: none -> 8.45 us  [body(): pick_table = jnp.concatenate(lax.all_to_all(sent, 'ctx', 0, 0), axis=0)]
  transfers between devices with their start and end apart: 1 -> 2, of which waited for: 1 -> 2; matrix products, arithmetic and copies ran while one was open for 0% -> 1% of each run, Pallas kernels for 0% -> 0%
where the time goes in v1:
time: 295 us
  waiting for transfers between devices  194 us (66%)
  blocking collectives  36.1 us (12%)
  local copies, waits for them, and re-layouts  27.3 us (9%)
  starting transfers between devices  20.4 us (7%)
  matrix products  10.1 us (3%)
  other arithmetic  6.99 us (2%)
    all_to_all x1, waiting for transfers between devices, body(): lax.all_to_all(outgoing, 'ctx', split_axis=0, concat_axis=0, tiled=True)  185 us
    all_to_all x1, blocking collectives, body(): lax.all_to_all(attended, 'kvh', split_axis=0, concat_axis=1, tiled=True)  36.1 us
    all_to_all x1, starting transfers between devices, body(): pick_table = jnp.concatenate(lax.all_to_all(sent, 'ctx', 0, 0), axis=0)  14.8 us
    all_to_all x1, waiting for transfers between devices, body(): pick_table = jnp.concatenate(lax.all_to_all(sent, 'ctx', 0, 0), axis=0)  8.45 us
    gather x1, local copies, waits for them, and re-layouts, body(): outgoing = local_kv[wanted]  6.3 us
  transfers between devices with their start and end apart: 2, of which 2 were waited for; matrix products, arithmetic and copies ran while one was open for 1% of the time, Pallas kernels for 0%

profile of v1, /device:TPU:1, one launch (start us, length us, event | category | flops | bytes accessed | tf_op | source)
XLA Modules:
  0.0 294.9 jit_solution(17130398000729972316)
XLA Ops:
  0.0 1.4 stack.2
  1.4 14.8 %all-to-all-start = ((s32[64,4,8]{2,1,0:T(4,128)}), s32[64,4,8]{2,1,0:T(4,128)S(1)}, u32[]{:S(2)}, u32[]{:S(2)}) async-start(s32[64,4,8]{2,1,0:T(4,128)} %stack.2), calls=%async_computation | async-start | bytes 262144 | tf_op jit(solution)/shard_map/all_to_all | solution.py:72
  16.2 0.9 constant_dynamic-update-slice_fusion.2
  17.1 0.9 constant_dynamic-update-slice_fusion.1
  18.1 8.5 %all-to-all-done = s32[64,4,8]{2,1,0:T(4,128)S(1)} async-done(((s32[64,4,8]{2,1,0:T(4,128)}), s32[64,4,8]{2,1,0:T(4,128)S(1)}, u32[]{:S(2)}, u32[]{:S(2)}) %all-to-all-start) | async-done | bytes 8224 | tf_op jit(solution)/shard_map/all_to_all | solution.py:72
  26.8 1.3 select_reduce_fusion
  28.2 2.6 fusion.19
  31.1 0.1 reshape.251
  31.2 6.3 %gather_fusion = bf16[128,128,256]{2,1,0:T(8,128)(2,1)} fusion(bf16[4,128,256]{2,1,0:T(8,128)(2,1)S(1)} %bitcast.107, s32[1024]{0:T(1024)S(1)} %pad_clamp_fusion.1), kind=kCustom, calls=%fused_computation | custom fusion | bytes 16777728 | tf_op jit(solution)/shard_map/gather | solution.py:80
  37.6 5.6 %all-to-all-start.1 = ((bf16[64,2,128,256]{3,2,1,0:T(8,128)(2,1)}), bf16[64,2,128,256]{3,2,1,0:T(8,128)(2,1)}, u32[]{:S(2)}, u32[]{:S(2)}) async-start(bf16[64,2,128,256]{3,2,1,0:T(8,128)(2,1)} %bitcast.109), calls=%async_computation.1 | async-start | bytes 16777216 | tf_op jit(solution)/shard_map/all_to_all | solution.py:81
  43.6 0.2 select_reduce_fusion.1
  43.8 185.2 %all-to-all-done.1 = bf16[64,2,128,256]{3,2,1,0:T(8,128)(2,1)} async-done(((bf16[64,2,128,256]{3,2,1,0:T(8,128)(2,1)}), bf16[64,2,128,256]{3,2,1,0:T(8,128)(2,1)}, u32[]{:S(2)}, u32[]{:S(2)}) %all-to-all-start.1) | async-done | bytes 8388640 | tf_op jit(solution)/shard_map/all_to_all | solution.py:81
  229.0 5.4 %gather_fusion.1 = bf16[28,128,256]{2,1,0:T(8,128)(2,1)} fusion(bf16[128,128,256]{2,1,0:T(8,128)(2,1)} %bitcast.21, s32[1024]{0:T(1024)S(1)} %pad_clamp_fusion), kind=kCustom, calls=%fused_computation.1 | custom fusion | bytes 3670128 | tf_op jit(solution)/shard_map/gather | solution.py:83
  234.3 1.7 pad_maximum_fusion
  236.0 21.8 %while.11 = (s32[]{:T(128)}, bf16[4,128,1024]{2,1,0:T(8,128)(2,1)}, bf16[4,8,128,256]{3,2,1,0:T(8,128)(2,1)S(1)}, bf16[4,128,1024]{2,1,0:T(8,128)(2,1)}, s32[]{:T(128)}, /*index=5*/pred[]{:T(512)}) while((s32[]{:T(128)}, bf16[4,128,1024]{2,1,0:T(8,128)(2,1)}, bf16[4,8,128,256]{3,2,1,0:T(8,128)(2,1)S(1)}, bf16[4,128,1024]{2,1,0:T(8,128)(2,1)}, ...), condition=%wide.region_7.8_spmd, body=%wide.region_4.7_spmd.sunk | while | flops 548681728 | bytes 19452492 | solution.py:92
  236.2 0.4 copy.68
  236.6 1.0 constant_dynamic-slice_fusion.4
  237.6 0.2 copy.67
  237.9 0.7 fusion.44
  238.6 0.9 fusion.45
  239.5 1.1 fusion.46
  240.6 0.1 copy.69
  240.8 0.7 constant_dynamic-update-slice_fusion.4
  241.7 0.4 copy.68
  242.1 1.0 constant_dynamic-slice_fusion.4
  243.1 0.2 copy.67
  243.3 0.7 fusion.44
  244.1 0.9 fusion.45
  244.9 1.1 fusion.46
  246.1 0.1 copy.69
  246.2 0.7 constant_dynamic-update-slice_fusion.4
  247.1 0.4 copy.68
  247.5 1.0 constant_dynamic-slice_fusion.4
  248.5 0.2 copy.67
  248.7 0.7 fusion.44
  249.5 0.9 fusion.45
  250.4 1.1 fusion.46
  251.5 0.1 copy.69
  251.6 0.7 constant_dynamic-update-slice_fusion.4
  252.5 0.4 copy.68
  253.0 1.0 constant_dynamic-slice_fusion.4
  253.9 0.2 copy.67
  254.2 0.7 fusion.44
  254.9 0.9 fusion.45
  255.8 1.1 fusion.46
  257.1 0.7 constant_dynamic-update-slice_fusion.4
  257.8 36.1 %all_to_all.29 = bf16[8,64,1024]{2,1,0:T(8,128)(2,1)S(1)} all-to-all(bf16[8,64,1024]{2,1,0:T(8,128)(2,1)} %bitcast.116), channel_id=1, replica_groups=mesh['ctx'=64,'kvh'=8] {'kvh'}, dimensions={0} | all-to-all | bytes 2097152 | tf_op jit(solution)/shard_map/all_to_all | solution.py:94
  293.9 1.1 copy.61
  (39 shorter events, 2.0 us)
Async XLA Ops:
  1.4 25.2 %all-to-all-start = ((s32[64,4,8]{2,1,0:T(4,128)}), s32[64,4,8]{2,1,0:T(4,128)S(1)}, u32[]{:S(2)}, u32[]{:S(2)}) async-start(s32[64,4,8]{2,1,0:T(4,128)} %stack.2), calls=%async_computation | async-start | bytes 262144 | tf_op jit(solution)/shard_map/all_to_all | solution.py:72
  37.6 5.6 %copy-start = (s32[4,8]{1,0:T(4,128)S(1)}, s32[4,8]{1,0:T(4,128)}, u32[]{:S(2)}) copy-start(s32[4,8]{1,0:T(4,128)} %param.9) | copy-start | bytes 388
  37.6 191.4 %all-to-all-start.1 = ((bf16[64,2,128,256]{3,2,1,0:T(8,128)(2,1)}), bf16[64,2,128,256]{3,2,1,0:T(8,128)(2,1)}, u32[]{:S(2)}, u32[]{:S(2)}) async-start(bf16[64,2,128,256]{3,2,1,0:T(8,128)(2,1)} %bitcast.109), calls=%async_computation.1 | async-start | bytes 16777216 | tf_op jit(solution)/shard_map/all_to_all | solution.py:81
